TPU v7x, 512 devices: a whole 4x8x8 slice. The times are simulated.
512 devices in a mesh: seq: 128 (over y, z, core), head: 4 (over x).
Axes of the slice: x: 4, y: 8, z: 8, core: 2. Of those that a mesh axis runs over, the one named last changes fastest.
Arguments:
- tokens: bfloat16 [16384, 2048], P('seq', 'head'), as said below
- w_query: bfloat16 [2048, 1024], P(None, 'head'), may hold values from -0.125 to 0.125
- w_key: bfloat16 [2048, 1024], P(None, 'head')
- w_value: bfloat16 [2048, 1024], P(None, 'head'), may hold values from -0.125 to 0.125
- gate_codes: int32 [16384, 8], P('seq', 'head'), may hold values from 28 to 1572854, as said below
- beta_codes: int32 [16384, 8], P('seq', 'head'), may hold values from 32 to 256
- norm_gain: float32 [128], replicated, may hold values from 0.25 to 1.75
- w_out: bfloat16 [1024, 2048], P('head'), may hold values from -0.1875 to 0.1875
Outputs:
- mixed: bfloat16 [16384, 2048], P('seq', 'head')
Inputs may be any that keep to these rules, and one draw needn't show every extreme that they name: `gate_codes`: codes are positive; the sweep's gates are those of one recording, identical law in every draw. `tokens`: activations of order one to ten.
All inputs are finite; a program needn't handle non-finite values.
Results may differ from a plain program's by a relative error of at most 0.0049.
Values may be sent and summed in bfloat16 or wider, within the bound.
A program may use at most 128 MiB of HBM per device.

v0:
```python
import jax
import jax.numpy as jnp
from jax import lax
from jax.sharding import PartitionSpec as P

SPAN = 64


def entering(part, axis, combine, identity):
    place = lax.axis_index(axis)
    gathered = jax.tree.map(lambda a: lax.all_gather(a, axis), part)
    state = jax.tree.map(lambda a, e: jnp.zeros_like(a) + jnp.asarray(e, a.dtype), part, identity)

    def one(step, state):
        return combine(
            state, jax.tree.map(lambda a: lax.dynamic_index_in_dim(a, step, 0, False), gathered)
        )

    return lax.fori_loop(0, place, one, state)


def shards(tokens, w_query, w_key, w_value, gate_codes, beta_codes, norm_gain, w_out):
    highest = lax.Precision.HIGHEST
    tok_rows = tokens.shape[0]
    heads_here = gate_codes.shape[1]
    head_size = norm_gain.shape[0]
    n_spans = tok_rows // SPAN
    piece = lax.all_gather(tokens, "head", axis=1, tiled=True)
    query, key_rows, value = tuple(
        (
            jnp.dot(piece, weight, preferred_element_type=jnp.float32)
            for weight in (w_query, w_key, w_value)
        )
    )

    def split_heads(array):
        return array.reshape(n_spans, SPAN, heads_here, head_size).transpose(2, 0, 1, 3)

    queries = split_heads(query)
    unit_keys = split_heads(key_rows)
    unit_keys = unit_keys * lax.rsqrt(jnp.sum(unit_keys * unit_keys, -1, keepdims=True) + 1e-06)
    values = split_heads(value)
    decay_log = (
        (-gate_codes.astype(jnp.float32) / 2097152.0)
        .reshape(n_spans, SPAN, heads_here)
        .transpose(2, 0, 1)
    )
    log_decay = jnp.cumsum(decay_log, axis=-1)
    betas = (
        (beta_codes.astype(jnp.float32) / 256.0)
        .reshape(n_spans, SPAN, heads_here)
        .transpose(2, 0, 1)
    )
    positions = jnp.arange(SPAN)
    lower_incl = positions[:, None] >= positions[None, :]
    lower_strict = positions[:, None] > positions[None, :]
    gaps = log_decay[..., :, None] - log_decay[..., None, :]
    inclusive = jnp.where(lower_incl, jnp.exp(jnp.where(lower_incl, gaps, 0.0)), 0.0)
    strict = jnp.where(lower_strict, inclusive, 0.0)
    key_dots = jnp.einsum("hctd,hcid->hcti", unit_keys, unit_keys, precision=highest)
    system = jnp.eye(SPAN, dtype=jnp.float32) + betas[..., :, None] * key_dots * strict
    right = jnp.concatenate(
        [betas[..., None] * unit_keys * jnp.exp(log_decay)[..., None], betas[..., None] * values],
        axis=-1,
    )
    solved = jax.scipy.linalg.solve_triangular(system, right, lower=True, unit_diagonal=True)
    wy_keys = solved[..., :head_size]
    wy_values = solved[..., head_size:]
    query_dots = jnp.einsum("hctd,hcid->hcti", queries, unit_keys, precision=highest) * inclusive
    intra = jnp.einsum("hcti,hciv->hctv", query_dots, wy_values, precision=highest)
    query_eff = queries * jnp.exp(log_decay)[..., None] - jnp.einsum(
        "hcti,hcik->hctk", query_dots, wy_keys, precision=highest
    )
    last_log = log_decay[..., -1]
    key_tail = unit_keys * jnp.exp(last_log[..., None] - log_decay)[..., None]
    identity_mat = jnp.eye(head_size, dtype=jnp.float32)
    span_maps = jnp.exp(last_log)[..., None, None] * identity_mat - jnp.einsum(
        "hctk,hctj->hckj", wy_keys, key_tail, precision=highest
    )
    span_adds = jnp.einsum("hctv,hctk->hcvk", wy_values, key_tail, precision=highest)
    span_maps = jnp.moveaxis(span_maps, 1, 0)
    span_adds = jnp.moveaxis(span_adds, 1, 0)
    zero_state = jnp.zeros((heads_here, head_size, head_size), jnp.float32)
    unit_maps = jnp.broadcast_to(identity_mat, (heads_here, head_size, head_size))

    def advance(carry, inputs):
        state, product = carry
        step_map, step_add = inputs
        new_state = jnp.einsum("hvk,hkj->hvj", state, step_map, precision=highest) + step_add
        new_product = jnp.einsum("hik,hkj->hij", product, step_map, precision=highest)
        return ((new_state, new_product), (state, product))

    def summarize(carry, inputs):
        new_carry, _ = advance(carry, inputs)
        return (new_carry, None)

    def combine(earlier, later):
        return (
            jnp.einsum("hik,hkj->hij", earlier[0], later[0], precision=highest),
            jnp.einsum("hvk,hkj->hvj", earlier[1], later[0], precision=highest) + later[1],
        )

    (summary_state, summary_map), _ = lax.scan(
        summarize, (zero_state, unit_maps), (span_maps, span_adds)
    )
    _, incoming = entering((summary_map, summary_state), "seq", combine, (unit_maps, zero_state))

    def replay(state, inputs):
        step_map, step_add = inputs
        return (jnp.einsum("hvk,hkj->hvj", state, step_map, precision=highest) + step_add, state)

    _, starts = lax.scan(replay, incoming, (span_maps, span_adds))
    outputs = intra + jnp.einsum("hctk,chvk->hctv", query_eff, starts, precision=highest)
    normed = outputs * lax.rsqrt(jnp.mean(outputs * outputs, -1, keepdims=True) + 1e-06) * norm_gain
    normed = (
        normed.astype(jnp.bfloat16).transpose(1, 2, 0, 3).reshape(tok_rows, heads_here * head_size)
    )
    partial_out = jnp.dot(normed, w_out, preferred_element_type=jnp.float32)
    return lax.psum_scatter(partial_out, "head", scatter_dimension=1, tiled=True).astype(
        jnp.bfloat16
    )


def solution(mesh):
    return jax.shard_map(
        shards,
        mesh=mesh,
        in_specs=(
            P("seq", "head"),
            P(None, "head"),
            P(None, "head"),
            P(None, "head"),
            P("seq", "head"),
            P("seq", "head"),
            P(),
            P("head", None),
        ),
        out_specs=P("seq", "head"),
        check_vma=False,
    )
```

profile of v0, /device:TPU:8, one launch (start us, length us, event | category | flops | bytes accessed | tf_op | source)
XLA Modules:
  0.0 591.1 jit_solution(8923890875720144227)
XLA Ops:
  8.2 13.3 %all_gather.15 = bf16[128,2048]{1,0:T(8,128)(2,1)S(1)} all-gather(bf16[128,512]{1,0:T(8,128)(2,1)} %param.14), channel_id=1, replica_groups=mesh['seq'=128,'head'=4] {'head'}, dimensions={1}, use_global_device_ids=true | all-gather | bytes 655360 | tf_op jit(solution)/shard_map/all_gather | solution.py:28
  21.5 1.5 fusion.56
  24.0 1.5 fusion.57
  26.2 19.7 %custom-call.4 = f32[2,2,1,64,64]{3,4,2,1,0:T(8,128)S(1)} custom-call(f32[2,2,1,64,64]{4,3,2,1,0:T(8,128)S(1)} %fusion.24), custom_call_target="InvertDiagBlocksLowerTriangular" | custom-call | tf_op jit(solution)/shard_map/jit(_solve_triangular)/vmap(vmap())/triangular_solve | solution.py:66
  48.2 1.2 while.39
  51.1 1.5 fusion.55
  53.7 101.4 %all-gather.5.cloned.1.call-done = f32[256,128,128]{2,1,0:T(8,128)} async-done(((f32[2,128,128]{2,1,0:T(8,128)}), f32[256,128,128]{2,1,0:T(8,128)}) %all-gather.5.cloned.1.call-update) | async-done | bytes 16777232 | tf_op jit(solution)/shard_map/all_gather | solution.py:11
  155.1 101.3 %all-gather.7.cloned.1.call-done = f32[256,128,128]{2,1,0:T(8,128)} async-done(((f32[2,128,128]{2,1,0:T(8,128)}), f32[256,128,128]{2,1,0:T(8,128)}) %all-gather.7.cloned.1.call-update) | async-done | bytes 16777232 | tf_op jit(solution)/shard_map/all_gather | solution.py:11
  256.4 37.9 %while.37 = (s32[]{:T(128)}, f32[2,128,128]{1,2,0:T(8,128)S(1)}, s32[]{:T(128)}, f32[128,2,128,128]{3,2,1,0:T(8,128)}, f32[128,2,128,128]{3,2,1,0:T(8,128)}, /*index=5*/s32[]{:T(128)}, s32[]{:T(128)}, s32[]{:T(128)}) while((s32[]{:T(128)}, f32[2,128,128]{1,2,0:T(8,128)S(1)}, s32[]{:T(128)}, f32[128,2,128,128]{3,2,1,0:T(8,128)}, ...), condition=%wide.region_5.6_spmd, body=%wide.region_4.5_spmd.sunk | while | flops 50364420 | bytes 1310855 | solution.py:19
  256.5 0.9 constant_dynamic-slice_fusion.2
  257.5 1.3 fusion.85
  258.8 0.9 constant_dynamic-slice_fusion.2
  259.9 1.3 fusion.85
  261.2 0.9 constant_dynamic-slice_fusion.2
  262.2 1.3 fusion.85
  264.6 1.3 fusion.85
  267.0 1.3 fusion.85
  269.3 1.3 fusion.85
  271.7 1.3 fusion.85
  274.1 1.3 fusion.85
  276.4 1.3 fusion.85
  278.8 1.3 fusion.85
  281.2 1.3 fusion.85
  283.5 1.3 fusion.85
  285.9 1.3 fusion.85
  287.3 0.9 constant_dynamic-slice_fusion.2
  288.3 1.3 fusion.85
  290.7 1.3 fusion.85
  293.0 1.3 fusion.85
  295.7 1.3 fusion.42
  297.0 286.0 %reduce-scatter.2.cloned.1.call-done = f32[128,512]{1,0:T(8,128)} async-done(((f32[128,2048]{1,0:T(8,128)}), f32[128,512]{1,0:T(8,128)}) %reduce-scatter.2.cloned.1.call-update) | async-done | bytes 262160 | tf_op jit(solution)/shard_map/reduce_scatter | solution.py:119
  582.9 1.6 convert_element_type.34
  (108 shorter events, 23.8 us)
Async XLA Ops:
  6.5 289.1 %copy-start = (bf16[256,2048]{1,0:T(8,128)(2,1)S(1)}, bf16[256,2048]{1,0:T(8,128)(2,1)}, u32[]{:S(2)}) copy-start(bf16[256,2048]{1,0:T(8,128)(2,1)} %param.21) | copy-start | bytes 3145732
  6.5 148.5 %all-gather.5.cloned.1.call-start = ((), (), s32[]{:S(2)}) async-start(), calls=%async_computation.2 | async-start | bytes 16908288 | tf_op jit(solution)/shard_map/all_gather | solution.py:11
  7.5 288.0 %copy-start.1 = (f32[128]{0:T(128)S(1)}, f32[128]{0:T(128)}, u32[]{:S(2)}) copy-start(f32[128]{0:T(128)} %param.20) | copy-start | bytes 1540
  50.2 206.2 %all-gather.7.cloned.1.call-start = ((), (), s32[]{:S(2)}) async-start(), calls=%async_computation.3 | async-start | bytes 16908288 | tf_op jit(solution)/shard_map/all_gather | solution.py:11
  51.1 531.9 %reduce-scatter.2.cloned.1.call-start = ((), (), s32[]{:S(2)}) async-start(), calls=%async_computation.1 | async-start | bytes 1310720 | tf_op jit(solution)/shard_map/reduce_scatter | solution.py:119
Sparse Core Ops, SparseCore 0:
  50.4 104.6 all-gather.4
  158.2 98.1 all-gather.6
  297.1 285.7 reduce-scatter.1
where the time goes:
time: 596 us; the launch traced here: 591 us
  waiting for transfers between devices  489 us (82%)
  matrix products  31.8 us (5%)
  other arithmetic  23.8 us (4%)
  local copies, waits for them, and re-layouts  19 us (3%)
  between operations  13.4 us (2%)
  blocking collectives  13.3 us (2%)
    reduce_scatter x1, waiting for transfers between devices, shards(): lax.psum_scatter(partial_out, 'head', scatter_dimension=1, tiled=True)  286 us
    all_gather x2, waiting for transfers between devices, entering(): gathered = jax.tree.map(lambda a: lax.all_gather(a, axis), part)  203 us
    dot_general x16, matrix products, combine(): jnp.einsum('hvk,hkj->hvj', earlier[1], later[0], precision=highest)  20.7 us
    another operation x3, other arithmetic, shards(): jax.scipy.linalg.solve_triangular(system, right, lower=True, unit_diagona...  19.7 us
    dynamic_slice x32, local copies, waits for them, and re-layouts, one(): lax.dynamic_index_in_dim(a, step, 0, False)  16.2 us
    all_gather x1, blocking collectives, shards(): piece = lax.all_gather(tokens, 'head', axis=1, tiled=True)  13.3 us
  transfers between devices with their start and end apart: 3, of which 3 were waited for; matrix products, arithmetic and copies ran while one was open for 1% of the time, Pallas kernels for 0%

commit v1 on v0

--- a/solution.py
+++ b/solution.py
@@ -25,7 +25,9 @@
     heads_here = gate_codes.shape[1]
     head_size = norm_gain.shape[0]
     n_spans = tok_rows // SPAN
-    piece = lax.all_gather(tokens, "head", axis=1, tiled=True)
+    piece = jnp.concatenate(
+        lax.all_to_all(jnp.stack([tokens] * lax.axis_size("head")), "head", 0, 0), axis=1
+    )
     query, key_rows, value = tuple(
         (
             jnp.dot(piece, weight, preferred_element_type=jnp.float32)

time: 596 us -> 600 us (level)
  blocking collectives: 13.3 us -> 0 us
  local copies, waits for them, and re-layouts: 19 us -> 30.9 us
    all_gather x1 -> x0, blocking collectives: 13.3 us -> none  [shards(): piece = lax.all_gather(tokens, 'head', axis=1, tiled=True)]
    dot_general x0 -> x4, local copies, waits for them, and re-layouts: none -> 6.65 us  [shards(): jnp.dot(piece, weight, preferred_element_type=jnp.float32)]
  transfers between devices with their start and end apart: 3 -> 4, of which waited for: 3 -> 4; matrix products, arithmetic and copies ran while one was open for 1% -> 2% of each run, Pallas kernels for 0% -> 0%
where the time goes in v1:
time: 600 us; the launch traced here: 595 us
  waiting for transfers between devices  488 us (81%)
  matrix products  32.8 us (5%)
  local copies, waits for them, and re-layouts  30.9 us (5%)
  other arithmetic  25 us (4%)
  between operations  13.4 us (2%)
    reduce_scatter x1, waiting for transfers between devices, shards(): lax.psum_scatter(partial_out, 'head', scatter_dimension=1, tiled=True)  286 us
    all_gather x2, waiting for transfers between devices, entering(): gathered = jax.tree.map(lambda a: lax.all_gather(a, axis), part)  200 us
    dot_general x16, matrix products, combine(): jnp.einsum('hvk,hkj->hvj', earlier[1], later[0], precision=highest)  20.7 us
    another operation x3, other arithmetic, shards(): jax.scipy.linalg.solve_triangular(system, right, lower=True, unit_diagona...  19.7 us
    dynamic_slice x32, local copies, waits for them, and re-layouts, one(): lax.dynamic_index_in_dim(a, step, 0, False)  16.2 us
  transfers between devices with their start and end apart: 4, of which 4 were waited for; matrix products, arithmetic and copies ran while one was open for 2% of the time, Pallas kernels for 0%

profile of v1, /device:TPU:8, one launch (start us, length us, event | category | flops | bytes accessed | tf_op | source)
XLA Modules:
  0.0 595.4 jit_solution(337850250392734940)
XLA Ops:
  6.5 1.8 stack.2
  8.4 4.3 all-to-all-start
  15.7 2.3 copy.137
  17.9 1.5 copy.138
  20.1 2.1 all-to-all-done
  23.4 1.4 reshape.85
  24.8 1.8 multiply_reduce_fusion.1
  27.1 19.7 %custom-call.4 = f32[2,2,1,64,64]{3,4,2,1,0:T(8,128)S(1)} custom-call(f32[2,2,1,64,64]{4,3,2,1,0:T(8,128)S(1)} %fusion.25), custom_call_target="InvertDiagBlocksLowerTriangular" | custom-call | tf_op jit(solution)/shard_map/jit(_solve_triangular)/vmap(vmap())/triangular_solve | solution.py:68
  54.2 1.5 copy.136
  58.0 98.7 %all-gather.5.cloned.1.call-done = f32[256,128,128]{2,1,0:T(8,128)} async-done(((f32[2,128,128]{2,1,0:T(8,128)}), f32[256,128,128]{2,1,0:T(8,128)}) %all-gather.5.cloned.1.call-update) | async-done | bytes 16777232 | tf_op jit(solution)/shard_map/all_gather | solution.py:11
  156.7 101.3 %all-gather.7.cloned.1.call-done = f32[256,128,128]{2,1,0:T(8,128)} async-done(((f32[2,128,128]{2,1,0:T(8,128)}), f32[256,128,128]{2,1,0:T(8,128)}) %all-gather.7.cloned.1.call-update) | async-done | bytes 16777232 | tf_op jit(solution)/shard_map/all_gather | solution.py:11
  258.0 37.9 %while.37 = (s32[]{:T(128)}, f32[2,128,128]{1,2,0:T(8,128)S(1)}, s32[]{:T(128)}, f32[128,2,128,128]{3,2,1,0:T(8,128)}, f32[128,2,128,128]{3,2,1,0:T(8,128)}, /*index=5*/s32[]{:T(128)}, s32[]{:T(128)}, s32[]{:T(128)}) while((s32[]{:T(128)}, f32[2,128,128]{1,2,0:T(8,128)S(1)}, s32[]{:T(128)}, f32[128,2,128,128]{3,2,1,0:T(8,128)}, ...), condition=%wide.region_5.6_spmd, body=%wide.region_4.5_spmd.sunk | while | flops 50364420 | bytes 1310855 | solution.py:19
  259.1 1.3 fusion.79
  261.4 1.3 fusion.79
  263.8 1.3 fusion.79
  266.2 1.3 fusion.79
  268.5 1.3 fusion.79
  270.9 1.3 fusion.79
  273.3 1.3 fusion.79
  275.6 1.3 fusion.79
  278.0 1.3 fusion.79
  280.4 1.3 fusion.79
  282.7 1.3 fusion.79
  285.1 1.3 fusion.79
  287.5 1.3 fusion.79
  289.9 1.3 fusion.79
  292.2 1.3 fusion.79
  294.6 1.3 fusion.79
  295.9 1.9 while.38
  297.8 1.4 multiply_reduce_fusion
  301.4 285.8 %reduce-scatter.2.cloned.1.call-done = f32[128,512]{1,0:T(8,128)} async-done(((f32[128,2048]{1,0:T(8,128)}), f32[128,512]{1,0:T(8,128)}) %reduce-scatter.2.cloned.1.call-update) | async-done | bytes 262160 | tf_op jit(solution)/shard_map/reduce_scatter | solution.py:121
  587.2 1.6 convert_element_type.34
  (116 shorter events, 36.4 us)
Async XLA Ops:
  6.5 293.6 %copy-start = (bf16[256,2048]{1,0:T(8,128)(2,1)S(1)}, bf16[256,2048]{1,0:T(8,128)(2,1)}, u32[]{:S(2)}) copy-start(bf16[256,2048]{1,0:T(8,128)(2,1)} %param.21) | copy-start | bytes 3145732
  8.4 13.8 %all-to-all-start = ((bf16[4,128,512]{2,1,0:T(8,128)(2,1)}), bf16[4,128,512]{2,1,0:T(8,128)(2,1)S(1)}, u32[]{:S(2)}, u32[]{:S(2)}) async-start(bf16[4,128,512]{2,1,0:T(8,128)(2,1)} %stack.2), calls=%async_computation | async-start | bytes 1048576 | tf_op jit(solution)/shard_map/all_to_all | solution.py:29
  12.7 144.0 %all-gather.5.cloned.1.call-start = ((), (), s32[]{:S(2)}) async-start(), calls=%async_computation.3 | async-start | bytes 16908288 | tf_op jit(solution)/shard_map/all_gather | solution.py:11
  26.7 23.0 %copy-start.1 = (f32[2,2,64,128]{3,2,0,1:T(8,128)}, f32[2,2,64,128]{3,2,0,1:T(8,128)S(1)}, u32[]{:S(2)}) copy-start(f32[2,2,64,128]{3,2,0,1:T(8,128)S(1)} %get-tuple-element.207) | copy-start | bytes 393220
  53.3 204.6 %all-gather.7.cloned.1.call-start = ((), (), s32[]{:S(2)}) async-start(), calls=%async_computation.4 | async-start | bytes 16908288 | tf_op jit(solution)/shard_map/all_gather | solution.py:11
  54.1 533.1 %reduce-scatter.2.cloned.1.call-start = ((), (), s32[]{:S(2)}) async-start(), calls=%async_computation.2 | async-start | bytes 1310720 | tf_op jit(solution)/shard_map/reduce_scatter | solution.py:121
Sparse Core Ops, SparseCore 0:
  53.5 103.1 all-gather.4
  159.8 98.1 all-gather.6
  301.5 285.6 reduce-scatter.1
